TPU v7x, 32 devices: a whole 2x2x4 slice. The times are simulated.
32 devices in a mesh: wide: 8 (over z, x), narrow: 4 (over y, core).
Axes of the slice: x: 2, y: 2, z: 4, core: 2. Of those that a mesh axis runs over, the one named last changes fastest.
Arguments:
- tokens: bfloat16 [4096, 1024], P(('wide', 'narrow')), may hold values from -6 to 6
- cotangent: bfloat16 [4096, 1024], P(('wide', 'narrow')), may hold values from -6 to 6
- lengths: int32 [32], P(('wide', 'narrow')), may hold values from 8 to 128, as said below
- gain_attn: bfloat16 [2, 1024], P(None, 'narrow'), may hold values from 0.5 to 1.5
- w_query: bfloat16 [2, 1024, 1024], P(None, 'narrow'), may hold values from -0.1875 to 0.1875
- w_key: bfloat16 [2, 1024, 1024], P(None, 'narrow'), may hold values from -0.1875 to 0.1875
- w_value: bfloat16 [2, 1024, 1024], P(None, 'narrow'), may hold values from -0.1875 to 0.1875
- w_out: bfloat16 [2, 1024, 1024], P(None, 'narrow'), may hold values from -0.75 to 0.75
- gain_mlp: bfloat16 [2, 1024], P(None, 'narrow'), may hold values from 0.5 to 1.5
- w_gate: bfloat16 [2, 1024, 2816], P(None, 'narrow'), may hold values from -0.1875 to 0.1875
- w_up: bfloat16 [2, 1024, 2816], P(None, 'narrow'), may hold values from -0.1875 to 0.1875
- w_down: bfloat16 [2, 2816, 1024], P(None, 'narrow'), may hold values from -0.109375 to 0.109375
Outputs:
- output: bfloat16 [4096, 1024], P(('wide', 'narrow'))
- grad_tokens: float32 [4096, 1024], P(('wide', 'narrow'))
- grad_gain_attn: float32 [2, 1024], P(None, 'narrow')
- grad_w_query: float32 [2, 1024, 1024], P(None, 'narrow')
- grad_w_key: float32 [2, 1024, 1024], P(None, 'narrow')
- grad_w_value: float32 [2, 1024, 1024], P(None, 'narrow')
- grad_w_out: float32 [2, 1024, 1024], P(None, 'narrow')
- grad_gain_mlp: float32 [2, 1024], P(None, 'narrow')
- grad_w_gate: float32 [2, 1024, 2816], P(None, 'narrow')
- grad_w_up: float32 [2, 1024, 2816], P(None, 'narrow')
- grad_w_down: float32 [2, 2816, 1024], P(None, 'narrow')
Inputs may be any that keep to these rules, and one draw needn't show every extreme that they name: `lengths`: each slot's number of real tokens; positions at or beyond it are padding; in every draw one slot is full and one has the least length.
All inputs are finite; a program needn't handle non-finite values.
Results may differ from a plain program's by a relative error of at most 0.02.
Values may be sent and summed in bfloat16 or wider, within the bound.
A program may use at most 320 MiB of HBM per device.

v0:
```python
import math

import jax
import jax.numpy as jnp
from jax import lax
from jax.sharding import PartitionSpec as P

HEADS = 16
HEAD_DIM = 64


EPSILON = 1e-06
NEG_FILL = -1e30


def matmul(left, right):
    return jnp.dot(left, right, preferred_element_type=jnp.float32)


def contract_rows(left, right):
    return lax.dot_general(
        left, right, (((0,), (0,)), ((), ())), preferred_element_type=jnp.float32
    )


def times_flip(left, right):
    return lax.dot_general(
        left, right, (((1,), (1,)), ((), ())), preferred_element_type=jnp.float32
    )


def rms_parts(stream, gain):
    inverse = lax.rsqrt(jnp.mean(stream * stream, axis=-1, keepdims=True) + EPSILON)
    return (stream * inverse * gain, inverse)


def rms_back(stream, inverse, gain, grad_normed):
    scaled = grad_normed * gain
    grad_gain = jnp.sum(grad_normed * stream * inverse, axis=0)
    grad_stream = inverse * scaled - stream * inverse * inverse * inverse * jnp.mean(
        scaled * stream, axis=-1, keepdims=True
    )
    return (grad_stream, grad_gain)


def rotary_tables(seq_len):
    half_dim = HEAD_DIM // 2
    positions = jnp.arange(seq_len).astype(jnp.float32)
    frequency = jnp.exp(
        jnp.arange(half_dim).astype(jnp.float32) * (-2.0 * math.log(10000.0) / HEAD_DIM)
    )
    angles = positions[:, None] * frequency[None, :]
    angles = jnp.concatenate([angles, angles], axis=1)
    return (jnp.cos(angles)[:, None, :], jnp.sin(angles)[:, None, :])


def rotate(tensor, cos_table, sin_table):
    half_dim = tensor.shape[-1] // 2
    turned = jnp.concatenate([-tensor[..., half_dim:], tensor[..., :half_dim]], axis=-1)
    return tensor * cos_table + turned * sin_table


def rotate_back(grad_rot, cos_table, sin_table):
    half_dim = grad_rot.shape[-1] // 2
    with_sine = grad_rot * sin_table
    turned = jnp.concatenate([with_sine[..., half_dim:], -with_sine[..., :half_dim]], axis=-1)
    return grad_rot * cos_table + turned


def block_mask(start_row, block_rows, seq_len, length):
    query_pos = start_row + jnp.arange(block_rows)
    key_pos = jnp.arange(seq_len)
    return (key_pos[None, :] <= query_pos[:, None]) & (key_pos[None, :] < length)


def attention_forward(query_rows, key_rows, value_rows, length):
    seq_len = query_rows.shape[0]
    block_rows = min(512, seq_len)
    scaling = HEAD_DIM ** (-0.5)

    def one_block(block_index):
        start_row = block_index * block_rows
        scores = (
            jnp.einsum("qhd,khd->hqk", query_rows, key_rows, preferred_element_type=jnp.float32)
            * scaling
        )
        scores = jnp.where(
            block_mask(start_row, block_rows, seq_len, length)[None], scores, NEG_FILL
        )
        highest = jnp.max(scores, axis=-1, keepdims=True)
        exponent = jnp.exp(scores - highest)
        totals = jnp.sum(exponent, axis=-1, keepdims=True)
        weights_low = (exponent / totals).astype(jnp.bfloat16)
        attended = jnp.einsum(
            "hqk,khd->qhd", weights_low, value_rows, preferred_element_type=jnp.float32
        )
        return (attended, (highest + jnp.log(totals))[..., 0])

    attended, log_totals = lax.map(one_block, jnp.arange(seq_len // block_rows))
    return (attended.reshape(seq_len, HEADS * HEAD_DIM), log_totals)


def attention_backward(query_rows, key_rows, value_rows, log_totals, grad_attended, length):
    seq_len = query_rows.shape[0]
    block_rows = min(512, seq_len)
    scaling = HEAD_DIM ** (-0.5)

    def one_block(carry_grads, block_index):
        grad_keys, grad_values = carry_grads
        start_row = block_index * block_rows
        scores = (
            jnp.einsum("qhd,khd->hqk", query_rows, key_rows, preferred_element_type=jnp.float32)
            * scaling
        )
        scores = jnp.where(
            block_mask(start_row, block_rows, seq_len, length)[None], scores, NEG_FILL
        )
        weights_now = jnp.exp(scores - log_totals[block_index][:, :, None])
        grad_weights = jnp.einsum(
            "qhd,khd->hqk", grad_attended, value_rows, preferred_element_type=jnp.float32
        )
        grad_values = grad_values + jnp.einsum(
            "hqk,qhd->khd",
            weights_now.astype(jnp.bfloat16),
            grad_attended,
            preferred_element_type=jnp.float32,
        )
        inner_sum = jnp.sum(weights_now * grad_weights, axis=-1, keepdims=True)
        grad_scores = (weights_now * (grad_weights - inner_sum)).astype(jnp.bfloat16)
        grad_query = (
            jnp.einsum("hqk,khd->qhd", grad_scores, key_rows, preferred_element_type=jnp.float32)
            * scaling
        )
        grad_keys = (
            grad_keys
            + jnp.einsum(
                "hqk,qhd->khd", grad_scores, query_rows, preferred_element_type=jnp.float32
            )
            * scaling
        )
        return ((grad_keys, grad_values), grad_query)

    zero_grads = jnp.zeros(key_rows.shape, jnp.float32)
    (grad_keys, grad_values), grad_queries = lax.scan(
        one_block, (zero_grads, zero_grads), jnp.arange(seq_len // block_rows)
    )
    return (grad_queries.reshape(query_rows.shape), grad_keys, grad_values)


def layer_forward(stream, weights, first_values, length, cos_table, sin_table):
    gain_attn, w_query, w_key, w_value, w_out, gain_mlp, w_gate, w_up, w_down = weights
    seq_len = stream.shape[0]
    head_shape = (seq_len, HEADS, HEAD_DIM)
    normed_full, inverse_attn = rms_parts(stream, gain_attn.astype(jnp.float32))
    normed = normed_full.astype(jnp.bfloat16)
    query_rows = rotate(matmul(normed, w_query).reshape(head_shape), cos_table, sin_table).astype(
        jnp.bfloat16
    )
    key_rows = rotate(matmul(normed, w_key).reshape(head_shape), cos_table, sin_table).astype(
        jnp.bfloat16
    )
    value_rows = matmul(normed, w_value)
    if first_values is None:
        mixed_values = value_rows
    else:
        mixed_values = 0.5 * value_rows + 0.5 * first_values
    mixed_low = mixed_values.astype(jnp.bfloat16).reshape(head_shape)
    attended, log_totals = attention_forward(query_rows, key_rows, mixed_low, length)
    attended_low = attended.astype(jnp.bfloat16)
    middle = stream + matmul(attended_low, w_out)
    normed_mid_full, inverse_mlp = rms_parts(middle, gain_mlp.astype(jnp.float32))
    normed_mid = normed_mid_full.astype(jnp.bfloat16)
    gate_proj = matmul(normed_mid, w_gate)
    up_proj = matmul(normed_mid, w_up)
    hidden = (jax.nn.silu(gate_proj) * up_proj).astype(jnp.bfloat16)
    result = middle + matmul(hidden, w_down)
    saved = (
        inverse_attn,
        normed,
        query_rows,
        key_rows,
        mixed_low,
        log_totals,
        attended_low,
        middle,
        inverse_mlp,
        normed_mid,
        gate_proj,
        up_proj,
        hidden,
    )
    return (result, value_rows, saved)


def layer_backward(
    stream, weights, first_values, values_extra, length, cos_table, sin_table, grad_result
):
    gain_attn, w_query, w_key, w_value, w_out, gain_mlp, w_gate, w_up, w_down = weights
    result, value_rows, saved = layer_forward(
        stream, weights, first_values, length, cos_table, sin_table
    )
    (
        inverse_attn,
        normed,
        query_rows,
        key_rows,
        mixed_low,
        log_totals,
        attended_low,
        middle,
        inverse_mlp,
        normed_mid,
        gate_proj,
        up_proj,
        hidden,
    ) = saved
    seq_len = stream.shape[0]
    width = HEADS * HEAD_DIM
    head_shape = (seq_len, HEADS, HEAD_DIM)
    grad_result_low = grad_result.astype(jnp.bfloat16)
    grad_w_down = contract_rows(hidden, grad_result_low)
    grad_hidden = times_flip(grad_result_low, w_down)
    sigmoid_gate = jax.nn.sigmoid(gate_proj)
    grad_gate = (
        grad_hidden * up_proj * sigmoid_gate * (1.0 + gate_proj * (1.0 - sigmoid_gate))
    ).astype(jnp.bfloat16)
    grad_up = (grad_hidden * gate_proj * sigmoid_gate).astype(jnp.bfloat16)
    grad_w_gate = contract_rows(normed_mid, grad_gate)
    grad_w_up = contract_rows(normed_mid, grad_up)
    grad_normed_mid = times_flip(grad_gate, w_gate) + times_flip(grad_up, w_up)
    grad_middle, grad_gain_mlp = rms_back(
        middle, inverse_mlp, gain_mlp.astype(jnp.float32), grad_normed_mid
    )
    grad_middle = grad_middle + grad_result
    grad_middle_low = grad_middle.astype(jnp.bfloat16)
    grad_w_out = contract_rows(attended_low, grad_middle_low)
    grad_attended = times_flip(grad_middle_low, w_out).astype(jnp.bfloat16).reshape(head_shape)
    grad_query_rot, grad_key_rot, grad_mixed = attention_backward(
        query_rows, key_rows, mixed_low, log_totals, grad_attended, length
    )
    grad_query = (
        rotate_back(grad_query_rot, cos_table, sin_table)
        .reshape(seq_len, width)
        .astype(jnp.bfloat16)
    )
    grad_key = (
        rotate_back(grad_key_rot, cos_table, sin_table).reshape(seq_len, width).astype(jnp.bfloat16)
    )
    grad_mixed = grad_mixed.reshape(seq_len, width)
    if first_values is None:
        grad_value = (grad_mixed + values_extra).astype(jnp.bfloat16)
        extra_out = None
    else:
        grad_value = (0.5 * grad_mixed).astype(jnp.bfloat16)
        extra_out = 0.5 * grad_mixed
    grad_w_query = contract_rows(normed, grad_query)
    grad_w_key = contract_rows(normed, grad_key)
    grad_w_value = contract_rows(normed, grad_value)
    grad_normed = (
        times_flip(grad_query, w_query)
        + times_flip(grad_key, w_key)
        + times_flip(grad_value, w_value)
    )
    grad_stream, grad_gain_attn = rms_back(
        stream, inverse_attn, gain_attn.astype(jnp.float32), grad_normed
    )
    grad_stream = grad_stream + grad_middle
    grads = (
        grad_gain_attn,
        grad_w_query,
        grad_w_key,
        grad_w_value,
        grad_w_out,
        grad_gain_mlp,
        grad_w_gate,
        grad_w_up,
        grad_w_down,
    )
    return (grad_stream, grads, extra_out)


def fetch_layer(params, layer_index):
    return (
        lax.all_gather(params[0][layer_index], "narrow", axis=0, tiled=True),
        lax.all_gather(params[1][layer_index], "narrow", axis=0, tiled=True),
        lax.all_gather(params[2][layer_index], "narrow", axis=0, tiled=True),
        lax.all_gather(params[3][layer_index], "narrow", axis=0, tiled=True),
        lax.all_gather(params[4][layer_index], "narrow", axis=0, tiled=True),
        lax.all_gather(params[5][layer_index], "narrow", axis=0, tiled=True),
        lax.all_gather(params[6][layer_index], "narrow", axis=0, tiled=True),
        lax.all_gather(params[7][layer_index], "narrow", axis=0, tiled=True),
        lax.all_gather(params[8][layer_index], "narrow", axis=0, tiled=True),
    )


def arrange_rows(grad_full, narrow_size, wide_size):
    row_count = grad_full.shape[0]
    parts = grad_full.reshape(
        (narrow_size, wide_size, row_count // (narrow_size * wide_size)) + grad_full.shape[1:]
    )
    return jnp.swapaxes(parts, 0, 1).reshape(grad_full.shape)


def reduce_grads(grads):
    narrow_size = lax.axis_size("narrow")
    wide_size = lax.axis_size("wide")
    ordered = [arrange_rows(grad_full, narrow_size, wide_size) for grad_full in grads]
    pieces = (
        lax.psum_scatter(ordered[0], ("wide", "narrow"), scatter_dimension=0, tiled=True),
        lax.psum_scatter(ordered[1], ("wide", "narrow"), scatter_dimension=0, tiled=True),
        lax.psum_scatter(ordered[2], ("wide", "narrow"), scatter_dimension=0, tiled=True),
        lax.psum_scatter(ordered[3], ("wide", "narrow"), scatter_dimension=0, tiled=True),
        lax.psum_scatter(ordered[4], ("wide", "narrow"), scatter_dimension=0, tiled=True),
        lax.psum_scatter(ordered[5], ("wide", "narrow"), scatter_dimension=0, tiled=True),
        lax.psum_scatter(ordered[6], ("wide", "narrow"), scatter_dimension=0, tiled=True),
        lax.psum_scatter(ordered[7], ("wide", "narrow"), scatter_dimension=0, tiled=True),
        lax.psum_scatter(ordered[8], ("wide", "narrow"), scatter_dimension=0, tiled=True),
    )
    return (
        lax.all_gather(pieces[0].astype(jnp.bfloat16), "wide", axis=0, tiled=True).astype(
            jnp.float32
        ),
        lax.all_gather(pieces[1].astype(jnp.bfloat16), "wide", axis=0, tiled=True).astype(
            jnp.float32
        ),
        lax.all_gather(pieces[2].astype(jnp.bfloat16), "wide", axis=0, tiled=True).astype(
            jnp.float32
        ),
        lax.all_gather(pieces[3].astype(jnp.bfloat16), "wide", axis=0, tiled=True).astype(
            jnp.float32
        ),
        lax.all_gather(pieces[4].astype(jnp.bfloat16), "wide", axis=0, tiled=True).astype(
            jnp.float32
        ),
        lax.all_gather(pieces[5].astype(jnp.bfloat16), "wide", axis=0, tiled=True).astype(
            jnp.float32
        ),
        lax.all_gather(pieces[6].astype(jnp.bfloat16), "wide", axis=0, tiled=True).astype(
            jnp.float32
        ),
        lax.all_gather(pieces[7].astype(jnp.bfloat16), "wide", axis=0, tiled=True).astype(
            jnp.float32
        ),
        lax.all_gather(pieces[8].astype(jnp.bfloat16), "wide", axis=0, tiled=True).astype(
            jnp.float32
        ),
    )


def shards(
    tokens,
    cotangent,
    lengths,
    gain_attn,
    w_query,
    w_key,
    w_value,
    w_out,
    gain_mlp,
    w_gate,
    w_up,
    w_down,
):
    params = (gain_attn, w_query, w_key, w_value, w_out, gain_mlp, w_gate, w_up, w_down)
    seq_len = tokens.shape[0]
    length = lengths[0]
    cos_table, sin_table = rotary_tables(seq_len)
    start_stream = tokens.astype(jnp.float32)
    first_weights = fetch_layer(params, 0)
    mid_stream, first_values, unused_saved = layer_forward(
        start_stream, first_weights, None, length, cos_table, sin_table
    )
    second_weights = fetch_layer(params, 1)
    final_stream, unused_values, unused_later = layer_forward(
        mid_stream, second_weights, first_values, length, cos_table, sin_table
    )
    valid_rows = (jnp.arange(seq_len) < length).astype(jnp.float32)[:, None]
    grad_final = cotangent.astype(jnp.float32) * valid_rows
    second_back = fetch_layer(params, 1)
    grad_mid, grads_two, values_extra = layer_backward(
        mid_stream, second_back, first_values, None, length, cos_table, sin_table, grad_final
    )
    reduced_two = reduce_grads(grads_two)
    first_back = fetch_layer(params, 0)
    grad_start, grads_one, unused_extra = layer_backward(
        start_stream, first_back, None, values_extra, length, cos_table, sin_table, grad_mid
    )
    reduced_one = reduce_grads(grads_one)
    stacked = [
        jnp.stack([one_part, two_part]) for one_part, two_part in zip(reduced_one, reduced_two)
    ]
    return (
        final_stream.astype(jnp.bfloat16),
        grad_start,
        stacked[0],
        stacked[1],
        stacked[2],
        stacked[3],
        stacked[4],
        stacked[5],
        stacked[6],
        stacked[7],
        stacked[8],
    )


def solution(mesh):
    return jax.shard_map(
        shards,
        mesh=mesh,
        in_specs=(
            P(("wide", "narrow"), None),
            P(("wide", "narrow"), None),
            P(("wide", "narrow")),
            P(None, "narrow"),
            P(None, "narrow", None),
            P(None, "narrow", None),
            P(None, "narrow", None),
            P(None, "narrow", None),
            P(None, "narrow"),
            P(None, "narrow", None),
            P(None, "narrow", None),
            P(None, "narrow", None),
        ),
        out_specs=(
            P(("wide", "narrow"), None),
            P(("wide", "narrow"), None),
            P(None, "narrow"),
            P(None, "narrow", None),
            P(None, "narrow", None),
            P(None, "narrow", None),
            P(None, "narrow", None),
            P(None, "narrow"),
            P(None, "narrow", None),
            P(None, "narrow", None),
            P(None, "narrow", None),
        ),
        check_vma=False,
    )
```

profile of v0, /device:TPU:0, one launch (start us, length us, event | category | flops | bytes accessed | tf_op | source)
XLA Modules:
  0.0 2853.6 jit_solution(16091714350005740210)
XLA Ops:
  27.1 6.3 all-gather
  62.3 21.6 all-gather.53.cloned.1.call-done
  88.2 19.7 all-gather.57.cloned.1.call-done
  110.1 43.1 %all-gather.59.cloned.1.call-done = bf16[1,1024,2816]{2,1,0:T(8,128)(2,1)} async-done(((bf16[1,256,2816]{2,1,0:T(8,128)(2,1)}), bf16[1,1024,2816]{2,1,0:T(8,128)(2,1)}) %all-gather.59.cloned.1.call-update) | async-done | bytes 5767184 | tf_op jit(solution)/shard_map/all_gather | solution.py:290
  157.9 40.7 %all-gather.61.cloned.1.call-done = bf16[1,1024,2816]{2,1,0:T(8,128)(2,1)} async-done(((bf16[1,256,2816]{2,1,0:T(8,128)(2,1)}), bf16[1,1024,2816]{2,1,0:T(8,128)(2,1)}) %all-gather.61.cloned.1.call-update) | async-done | bytes 5767184 | tf_op jit(solution)/shard_map/all_gather | solution.py:291
  204.2 40.0 %all-gather.63.cloned.1.call-done = bf16[1,2816,1024]{2,1,0:T(8,128)(2,1)} async-done(((bf16[1,704,1024]{2,1,0:T(8,128)(2,1)}), bf16[1,2816,1024]{2,1,0:T(8,128)(2,1)}) %all-gather.63.cloned.1.call-update) | async-done | bytes 5767184 | tf_op jit(solution)/shard_map/all_gather | solution.py:292
  248.2 20.7 all-gather.65.cloned.1.call-done
  271.8 21.3 all-gather.69.cloned.1.call-done
  296.3 20.7 all-gather.67.cloned.1.call-done
  322.2 19.0 all-gather.71.cloned.1.call-done
  344.3 42.3 %all-gather.75.cloned.1.call-done = bf16[1,1024,2816]{2,1,0:T(8,128)(2,1)} async-done(((bf16[1,256,2816]{2,1,0:T(8,128)(2,1)}), bf16[1,1024,2816]{2,1,0:T(8,128)(2,1)}) %all-gather.75.cloned.1.call-update) | async-done | bytes 5767184 | tf_op jit(solution)/shard_map/all_gather | solution.py:291
  391.4 40.8 %all-gather.77.cloned.1.call-done = bf16[1,2816,1024]{2,1,0:T(8,128)(2,1)} async-done(((bf16[1,704,1024]{2,1,0:T(8,128)(2,1)}), bf16[1,2816,1024]{2,1,0:T(8,128)(2,1)}) %all-gather.77.cloned.1.call-update) | async-done | bytes 5767184 | tf_op jit(solution)/shard_map/all_gather | solution.py:292
  438.4 39.1 %all-gather.73.cloned.1.call-done = bf16[1,1024,2816]{2,1,0:T(8,128)(2,1)} async-done(((bf16[1,256,2816]{2,1,0:T(8,128)(2,1)}), bf16[1,1024,2816]{2,1,0:T(8,128)(2,1)}) %all-gather.73.cloned.1.call-update) | async-done | bytes 5767184 | tf_op jit(solution)/shard_map/all_gather | solution.py:290
  489.5 9.8 copy.186
  535.0 9.7 copy.185
  545.7 7.1 fusion.179
  552.8 9.9 copy.188
  562.7 7.0 fusion.178
  569.7 10.0 copy.187
  580.7 7.0 fusion.148
  587.7 11.2 copy.190
  660.8 11.2 copy.189
  673.9 137.3 %reduce-scatter.31.cloned.1.call-done = f32[32,2816]{1,0:T(8,128)} async-done(((f32[1024,2816]{1,0:T(8,128)}), f32[32,2816]{1,0:T(8,128)}) %reduce-scatter.31.cloned.1.call-update) | async-done | bytes 360464 | tf_op jit(solution)/shard_map/reduce_scatter | solution.py:315
  812.9 155.1 %reduce-scatter.37.cloned.1.call-done = f32[32,2816]{1,0:T(8,128)} async-done(((f32[1024,2816]{1,0:T(8,128)}), f32[32,2816]{1,0:T(8,128)}) %reduce-scatter.37.cloned.1.call-update) | async-done | bytes 360464 | tf_op jit(solution)/shard_map/reduce_scatter | solution.py:316
  969.8 154.5 %reduce-scatter.35.cloned.1.call-done = f32[32,2816]{1,0:T(8,128)} async-done(((f32[1024,2816]{1,0:T(8,128)}), f32[32,2816]{1,0:T(8,128)}) %reduce-scatter.35.cloned.1.call-update) | async-done | bytes 360464 | tf_op jit(solution)/shard_map/reduce_scatter | solution.py:316
  1126.1 155.0 %reduce-scatter.41.cloned.1.call-done = f32[88,1024]{1,0:T(8,128)} async-done(((f32[2816,1024]{1,0:T(8,128)}), f32[88,1024]{1,0:T(8,128)}) %reduce-scatter.41.cloned.1.call-update) | async-done | bytes 360464 | tf_op jit(solution)/shard_map/reduce_scatter | solution.py:317
  1284.7 38.4 %all-reduce.8 = (bf16[1024]{0:T(1024)(128)(2,1)S(1)}, bf16[1024]{0:T(1024)(128)(2,1)S(1)}, bf16[1024]{0:T(1024)(128)(2,1)S(1)}, bf16[1024]{0:T(1024)(128)(2,1)S(1)}) all-reduce(f32[1024]{0:T(1024)S(1)} %reshape.380, f32[1024]{0:T(1024)S(1)} %reshape.378, ...), channel_id=21, replica_groups=mesh['wide'=8,'narrow'=4] {'wide','narrow'}, use_global_device_ids=true, to_apply=%region_17.18.clone | all-reduce | flops 4096 | bytes 24576
  1324.3 20.3 all-reduce.9
  1350.0 75.7 %reduce-scatter.17.cloned.1.call-done = f32[32,1024]{1,0:T(8,128)} async-done(((f32[1024,1024]{1,0:T(8,128)}), f32[32,1024]{1,0:T(8,128)}) %reduce-scatter.17.cloned.1.call-update) | async-done | bytes 131088 | tf_op jit(solution)/shard_map/reduce_scatter | solution.py:310
  1426.6 140.5 %reduce-scatter.15.cloned.1.call-done = f32[32,1024]{1,0:T(8,128)} async-done(((f32[1024,1024]{1,0:T(8,128)}), f32[32,1024]{1,0:T(8,128)}) %reduce-scatter.15.cloned.1.call-update) | async-done | bytes 131088 | tf_op jit(solution)/shard_map/reduce_scatter | solution.py:310
  1568.0 140.4 %reduce-scatter.21.cloned.1.call-done = f32[32,1024]{1,0:T(8,128)} async-done(((f32[1024,1024]{1,0:T(8,128)}), f32[32,1024]{1,0:T(8,128)}) %reduce-scatter.21.cloned.1.call-update) | async-done | bytes 131088 | tf_op jit(solution)/shard_map/reduce_scatter | solution.py:311
  1709.4 139.7 %reduce-scatter.19.cloned.1.call-done = f32[32,1024]{1,0:T(8,128)} async-done(((f32[1024,1024]{1,0:T(8,128)}), f32[32,1024]{1,0:T(8,128)}) %reduce-scatter.19.cloned.1.call-update) | async-done | bytes 131088 | tf_op jit(solution)/shard_map/reduce_scatter | solution.py:311
  1850.0 139.5 %reduce-scatter.25.cloned.1.call-done = f32[32,1024]{1,0:T(8,128)} async-done(((f32[1024,1024]{1,0:T(8,128)}), f32[32,1024]{1,0:T(8,128)}) %reduce-scatter.25.cloned.1.call-update) | async-done | bytes 131088 | tf_op jit(solution)/shard_map/reduce_scatter | solution.py:312
  1990.5 139.7 %reduce-scatter.23.cloned.1.call-done = f32[32,1024]{1,0:T(8,128)} async-done(((f32[1024,1024]{1,0:T(8,128)}), f32[32,1024]{1,0:T(8,128)}) %reduce-scatter.23.cloned.1.call-update) | async-done | bytes 131088 | tf_op jit(solution)/shard_map/reduce_scatter | solution.py:312
  2131.1 139.6 %reduce-scatter.29.cloned.1.call-done = f32[32,1024]{1,0:T(8,128)} async-done(((f32[1024,1024]{1,0:T(8,128)}), f32[32,1024]{1,0:T(8,128)}) %reduce-scatter.29.cloned.1.call-update) | async-done | bytes 131088 | tf_op jit(solution)/shard_map/reduce_scatter | solution.py:313
  2271.6 139.6 %reduce-scatter.27.cloned.1.call-done = f32[32,1024]{1,0:T(8,128)} async-done(((f32[1024,1024]{1,0:T(8,128)}), f32[32,1024]{1,0:T(8,128)}) %reduce-scatter.27.cloned.1.call-update) | async-done | bytes 131088 | tf_op jit(solution)/shard_map/reduce_scatter | solution.py:313
  2412.1 31.9 %all_gather.147 = bf16[256,1024]{1,0:T(8,128)(2,1)S(1)} all-gather(bf16[32,1024]{1,0:T(8,128)(2,1)S(1)} %convert_element_type.363), channel_id=1, replica_groups=mesh['wide'=8,'narrow'=4] {'wide'}, dimensions={0}, use_global_device_ids=true | all-gather | bytes 589824 | tf_op jit(solution)/shard_map/all_gather | solution.py:323
  2444.0 31.8 %all_gather.146 = bf16[256,1024]{1,0:T(8,128)(2,1)S(1)} all-gather(bf16[32,1024]{1,0:T(8,128)(2,1)S(1)} %convert_element_type.362), channel_id=1, replica_groups=mesh['wide'=8,'narrow'=4] {'wide'}, dimensions={0}, use_global_device_ids=true | all-gather | bytes 589824 | tf_op jit(solution)/shard_map/all_gather | solution.py:323
  2475.8 31.8 %all_gather.149 = bf16[256,1024]{1,0:T(8,128)(2,1)S(1)} all-gather(bf16[32,1024]{1,0:T(8,128)(2,1)S(1)} %convert_element_type.365), channel_id=1, replica_groups=mesh['wide'=8,'narrow'=4] {'wide'}, dimensions={0}, use_global_device_ids=true | all-gather | bytes 589824 | tf_op jit(solution)/shard_map/all_gather | solution.py:326
  2507.6 31.5 %all_gather.148 = bf16[256,1024]{1,0:T(8,128)(2,1)S(1)} all-gather(bf16[32,1024]{1,0:T(8,128)(2,1)S(1)} %convert_element_type.364), channel_id=1, replica_groups=mesh['wide'=8,'narrow'=4] {'wide'}, dimensions={0}, use_global_device_ids=true | all-gather | bytes 589824 | tf_op jit(solution)/shard_map/all_gather | solution.py:326
  2539.2 30.5 %reduce-scatter.39.cloned.1.call-done = f32[88,1024]{1,0:T(8,128)} async-done(((f32[2816,1024]{1,0:T(8,128)}), f32[88,1024]{1,0:T(8,128)}) %reduce-scatter.39.cloned.1.call-update) | async-done | bytes 360464 | tf_op jit(solution)/shard_map/reduce_scatter | solution.py:317
  2574.3 32.6 %all_gather.151 = bf16[256,1024]{1,0:T(8,128)(2,1)S(1)} all-gather(bf16[32,1024]{1,0:T(8,128)(2,1)S(1)} %convert_element_type.367), channel_id=1, replica_groups=mesh['wide'=8,'narrow'=4] {'wide'}, dimensions={0}, use_global_device_ids=true | all-gather | bytes 589824 | tf_op jit(solution)/shard_map/all_gather | solution.py:329
  2606.9 32.4 %all_gather.150 = bf16[256,1024]{1,0:T(8,128)(2,1)S(1)} all-gather(bf16[32,1024]{1,0:T(8,128)(2,1)S(1)} %convert_element_type.366), channel_id=1, replica_groups=mesh['wide'=8,'narrow'=4] {'wide'}, dimensions={0}, use_global_device_ids=true | all-gather | bytes 589824 | tf_op jit(solution)/shard_map/all_gather | solution.py:329
  2640.8 32.9 %all_gather.153 = bf16[256,1024]{1,0:T(8,128)(2,1)S(1)} all-gather(bf16[32,1024]{1,0:T(8,128)(2,1)S(1)} %convert_element_type.369), channel_id=1, replica_groups=mesh['wide'=8,'narrow'=4] {'wide'}, dimensions={0}, use_global_device_ids=true | all-gather | bytes 589824 | tf_op jit(solution)/shard_map/all_gather | solution.py:332
  2673.6 31.8 %all_gather.152 = bf16[256,1024]{1,0:T(8,128)(2,1)S(1)} all-gather(bf16[32,1024]{1,0:T(8,128)(2,1)S(1)} %convert_element_type.368), channel_id=1, replica_groups=mesh['wide'=8,'narrow'=4] {'wide'}, dimensions={0}, use_global_device_ids=true | all-gather | bytes 589824 | tf_op jit(solution)/shard_map/all_gather | solution.py:332
  2711.6 42.6 %all-gather.43.cloned.1.call-done = bf16[256,2816]{1,0:T(8,128)(2,1)} async-done(((bf16[32,2816]{1,0:T(8,128)(2,1)}), bf16[256,2816]{1,0:T(8,128)(2,1)}) %all-gather.43.cloned.1.call-update) | async-done | bytes 1441808 | tf_op jit(solution)/shard_map/all_gather | solution.py:341
  2758.9 38.7 %all-gather.49.cloned.1.call-done = bf16[704,1024]{1,0:T(8,128)(2,1)} async-done(((bf16[88,1024]{1,0:T(8,128)(2,1)}), bf16[704,1024]{1,0:T(8,128)(2,1)}) %all-gather.49.cloned.1.call-update) | async-done | bytes 1441808 | tf_op jit(solution)/shard_map/all_gather | solution.py:344
  2797.7 44.2 %all-gather.47.cloned.1.call-done = bf16[704,1024]{1,0:T(8,128)(2,1)} async-done(((bf16[88,1024]{1,0:T(8,128)(2,1)}), bf16[704,1024]{1,0:T(8,128)(2,1)}) %all-gather.47.cloned.1.call-update) | async-done | bytes 1441808 | tf_op jit(solution)/shard_map/all_gather | solution.py:344
  (420 shorter events, 250.0 us)
Async XLA Ops:
  7.2 45.3 %all-gather.51.cloned.1.call-start = ((), (), s32[]{:S(2)}) async-start(), calls=%async_computation.34 | async-start | bytes 2621440 | tf_op jit(solution)/shard_map/all_gather | solution.py:287
  9.6 50.1 %all-gather.55.cloned.1.call-start = ((), (), s32[]{:S(2)}) async-start(), calls=%async_computation.36 | async-start | bytes 2621440 | tf_op jit(solution)/shard_map/all_gather | solution.py:286
  10.8 73.0 %all-gather.53.cloned.1.call-start = ((), (), s32[]{:S(2)}) async-start(), calls=%async_computation.35 | async-start | bytes 2621440 | tf_op jit(solution)/shard_map/all_gather | solution.py:285
  12.2 95.6 %all-gather.57.cloned.1.call-start = ((), (), s32[]{:S(2)}) async-start(), calls=%async_computation.37 | async-start | bytes 2621440 | tf_op jit(solution)/shard_map/all_gather | solution.py:288
  14.7 138.5 %all-gather.59.cloned.1.call-start = ((), (), s32[]{:S(2)}) async-start(), calls=%async_computation.38 | async-start | bytes 7208960 | tf_op jit(solution)/shard_map/all_gather | solution.py:290
  16.5 182.1 %all-gather.61.cloned.1.call-start = ((), (), s32[]{:S(2)}) async-start(), calls=%async_computation.39 | async-start | bytes 7208960 | tf_op jit(solution)/shard_map/all_gather | solution.py:291
  20.3 223.9 %all-gather.63.cloned.1.call-start = ((), (), s32[]{:S(2)}) async-start(), calls=%async_computation.40 | async-start | bytes 7208960 | tf_op jit(solution)/shard_map/all_gather | solution.py:292
  22.3 246.7 %all-gather.65.cloned.1.call-start = ((), (), s32[]{:S(2)}) async-start(), calls=%async_computation.41 | async-start | bytes 2621440 | tf_op jit(solution)/shard_map/all_gather | solution.py:287
  23.0 270.1 %all-gather.69.cloned.1.call-start = ((), (), s32[]{:S(2)}) async-start(), calls=%async_computation.43 | async-start | bytes 2621440 | tf_op jit(solution)/shard_map/all_gather | solution.py:286
  23.7 293.3 %all-gather.67.cloned.1.call-start = ((), (), s32[]{:S(2)}) async-start(), calls=%async_computation.42 | async-start | bytes 2621440 | tf_op jit(solution)/shard_map/all_gather | solution.py:285
  24.3 316.9 %all-gather.71.cloned.1.call-start = ((), (), s32[]{:S(2)}) async-start(), calls=%async_computation.44 | async-start | bytes 2621440 | tf_op jit(solution)/shard_map/all_gather | solution.py:288
  25.1 361.6 %all-gather.75.cloned.1.call-start = ((), (), s32[]{:S(2)}) async-start(), calls=%async_computation.46 | async-start | bytes 7208960 | tf_op jit(solution)/shard_map/all_gather | solution.py:291
  25.1 9.4 copy-start.83
  25.6 406.6 %all-gather.77.cloned.1.call-start = ((), (), s32[]{:S(2)}) async-start(), calls=%async_computation.47 | async-start | bytes 7208960 | tf_op jit(solution)/shard_map/all_gather | solution.py:292
  26.4 451.2 %all-gather.73.cloned.1.call-start = ((), (), s32[]{:S(2)}) async-start(), calls=%async_computation.45 | async-start | bytes 7208960 | tf_op jit(solution)/shard_map/all_gather | solution.py:290
  27.0 645.1 %reduce-scatter.33.cloned.1.call-start = ((), (), s32[]{:S(2)}) async-start(), calls=%async_computation.24 | async-start | bytes 11894784 | tf_op jit(solution)/shard_map/reduce_scatter | solution.py:315
  33.4 50.4 %copy-start.64 = (f32[1,1024]{1,0:T(1,128)}, f32[1,1024]{1,0:T(1,128)S(1)}, u32[]{:S(2)}) copy-start(f32[1,1024]{1,0:T(1,128)S(1)} %convert_element_type.378) | copy-start | bytes 12292
  33.6 50.3 %copy-start.75 = (f32[128]{0:T(128)}, f32[128]{0:T(128)S(1)}, u32[]{:S(2)}) copy-start(f32[128]{0:T(128)S(1)} %add_rsqrt_fusion.3) | copy-start | bytes 1540
  54.8 32.5 %copy-start.56 = (bf16[128,1024]{0,1:T(8,128)(2,1)}, bf16[128,1024]{0,1:T(8,128)(2,1)S(1)}, u32[]{:S(2)}) copy-start(bf16[128,1024]{0,1:T(8,128)(2,1)S(1)} %copy.149) | copy-start | bytes 786436
  88.1 69.7 %copy-start.61 = (bf16[16,64,128]{2,1,0:T(8,128)(2,1)}, bf16[16,64,128]{2,1,0:T(8,128)(2,1)S(1)}, u32[]{:S(2)}) copy-start(bf16[16,64,128]{2,1,0:T(8,128)(2,1)S(1)} %convolution_convert_fusion.1) | copy-start | bytes 786436
  88.2 21.8 copy-start.70
  110.0 134.2 %copy-start = (f32[128,1024]{1,0:T(8,128)}, f32[128,1024]{1,0:T(8,128)S(1)}, u32[]{:S(2)}) copy-start(f32[128,1024]{1,0:T(8,128)S(1)} %get-tuple-element.227) | copy-start | bytes 1572868
  110.0 47.9 %copy-start.80 = (f32[128]{0:T(128)}, f32[128]{0:T(128)S(1)}, u32[]{:S(2)}) copy-start(f32[128]{0:T(128)S(1)} %add_rsqrt_fusion.2) | copy-start | bytes 1540
  110.1 88.5 %copy-start.13 = (bf16[128,1024]{1,0:T(8,128)(2,1)}, bf16[128,1024]{1,0:T(8,128)(2,1)S(1)}, u32[]{:S(2)}) copy-start(bf16[128,1024]{1,0:T(8,128)(2,1)S(1)} %multiply_convert_fusion.10) | copy-start | bytes 786436
  248.1 20.8 copy-start.77
  322.2 21.2 copy-start.72
  344.3 87.9 %copy-start.79 = (f32[128]{0:T(128)S(1)}, f32[128]{0:T(128)}, u32[]{:S(2)}) copy-start(f32[128]{0:T(128)} %fusion.154) | copy-start | bytes 1540
  499.3 311.9 %reduce-scatter.31.cloned.1.call-start = ((), (), s32[]{:S(2)}) async-start(), calls=%async_computation.22 | async-start | bytes 11894784 | tf_op jit(solution)/shard_map/reduce_scatter | solution.py:315
  544.8 423.3 %reduce-scatter.37.cloned.1.call-start = ((), (), s32[]{:S(2)}) async-start(), calls=%async_computation.28 | async-start | bytes 11894784 | tf_op jit(solution)/shard_map/reduce_scatter | solution.py:316
  562.7 561.7 %reduce-scatter.35.cloned.1.call-start = ((), (), s32[]{:S(2)}) async-start(), calls=%async_computation.26 | async-start | bytes 11894784 | tf_op jit(solution)/shard_map/reduce_scatter | solution.py:316
  579.7 701.3 %reduce-scatter.41.cloned.1.call-start = ((), (), s32[]{:S(2)}) async-start(), calls=%async_computation.32 | async-start | bytes 11894784 | tf_op jit(solution)/shard_map/reduce_scatter | solution.py:317
  598.9 826.8 %reduce-scatter.17.cloned.1.call-start = ((), (), s32[]{:S(2)}) async-start(), calls=%async_computation.15 | async-start | bytes 4325376 | tf_op jit(solution)/shard_map/reduce_scatter | solution.py:310
  604.0 963.1 %reduce-scatter.15.cloned.1.call-start = ((), (), s32[]{:S(2)}) async-start(), calls=%async_computation.14 | async-start | bytes 4325376 | tf_op jit(solution)/shard_map/reduce_scatter | solution.py:310
  630.5 1078.0 %reduce-scatter.21.cloned.1.call-start = ((), (), s32[]{:S(2)}) async-start(), calls=%async_computation.17 | async-start | bytes 4325376 | tf_op jit(solution)/shard_map/reduce_scatter | solution.py:311
  634.5 1214.6 %reduce-scatter.19.cloned.1.call-start = ((), (), s32[]{:S(2)}) async-start(), calls=%async_computation.16 | async-start | bytes 4325376 | tf_op jit(solution)/shard_map/reduce_scatter | solution.py:311
  638.5 1351.1 %reduce-scatter.25.cloned.1.call-start = ((), (), s32[]{:S(2)}) async-start(), calls=%async_computation.19 | async-start | bytes 4325376 | tf_op jit(solution)/shard_map/reduce_scatter | solution.py:312
  642.5 1487.7 %reduce-scatter.23.cloned.1.call-start = ((), (), s32[]{:S(2)}) async-start(), calls=%async_computation.18 | async-start | bytes 4325376 | tf_op jit(solution)/shard_map/reduce_scatter | solution.py:312
  645.5 1625.1 %reduce-scatter.29.cloned.1.call-start = ((), (), s32[]{:S(2)}) async-start(), calls=%async_computation.21 | async-start | bytes 4325376 | tf_op jit(solution)/shard_map/reduce_scatter | solution.py:313
  649.5 1761.7 %reduce-scatter.27.cloned.1.call-start = ((), (), s32[]{:S(2)}) async-start(), calls=%async_computation.20 | async-start | bytes 4325376 | tf_op jit(solution)/shard_map/reduce_scatter | solution.py:313
  653.5 1916.2 %reduce-scatter.39.cloned.1.call-start = ((), (), s32[]{:S(2)}) async-start(), calls=%async_computation.30 | async-start | bytes 11894784 | tf_op jit(solution)/shard_map/reduce_scatter | solution.py:317
  672.0 610.8 %copy-start.84 = (u32[32]{0:T(128)S(1)}, u32[32]{0:T(128)}, u32[]{:S(2)}) copy-start(u32[32]{0:T(128)} %constant.143) | copy-start | bytes 388
  672.0 673.7 %copy-start.22 = (bf16[128,2816]{1,0:T(8,128)(2,1)S(1)}, bf16[128,2816]{1,0:T(8,128)(2,1)}, u32[]{:S(2)}) copy-start(bf16[128,2816]{1,0:T(8,128)(2,1)} %get-tuple-element.148) | copy-start | bytes 2162692
  672.0 2034.9 %all-gather.41.cloned.1.call-start = ((), (), s32[]{:S(2)}) async-start(), calls=%async_computation.25 | async-start | bytes 1622016 | tf_op jit(solution)/shard_map/all_gather | solution.py:338
  673.9 2033.0 %all-gather.39.cloned.1.call-start = ((), (), s32[]{:S(2)}) async-start(), calls=%async_computation.23 | async-start | bytes 1622016 | tf_op jit(solution)/shard_map/all_gather | solution.py:338
  812.9 1898.7 %all-gather.45.cloned.1.call-start = ((), (), s32[]{:S(2)}) async-start(), calls=%async_computation.29 | async-start | bytes 1622016 | tf_op jit(solution)/shard_map/all_gather | solution.py:341
  969.8 1784.5 %all-gather.43.cloned.1.call-start = ((), (), s32[]{:S(2)}) async-start(), calls=%async_computation.27 | async-start | bytes 1622016 | tf_op jit(solution)/shard_map/all_gather | solution.py:341
  1126.1 1671.6 %all-gather.49.cloned.1.call-start = ((), (), s32[]{:S(2)}) async-start(), calls=%async_computation.33 | async-start | bytes 1622016 | tf_op jit(solution)/shard_map/all_gather | solution.py:344
  1282.8 1559.0 %all-gather.47.cloned.1.call-start = ((), (), s32[]{:S(2)}) async-start(), calls=%async_computation.31 | async-start | bytes 1622016 | tf_op jit(solution)/shard_map/all_gather | solution.py:344
  (72 other events, 167.5 us)
Sparse Core Ops, SparseCore 0:
  10.1 25.2 all-gather.50
  37.0 22.5 all-gather.54
  61.2 22.5 all-gather.52
  85.2 22.5 all-gather.56
  109.8 43.3 all-gather.58
  155.2 43.3 all-gather.60
  200.8 43.3 all-gather.62
  246.3 22.5 all-gather.64
  270.5 22.5 all-gather.68
  294.5 22.5 all-gather.66
  318.6 22.5 all-gather.70
  343.2 43.3 all-gather.74
  388.8 43.3 all-gather.76
  434.2 43.3 all-gather.72
  499.4 155.0 reduce-scatter.32
  656.7 154.4 reduce-scatter.30
  813.3 154.6 reduce-scatter.36
  970.2 154.0 reduce-scatter.34
  1126.7 154.3 reduce-scatter.40
  1283.8 141.8 reduce-scatter.16
  1428.6 138.5 reduce-scatter.14
  1570.0 138.4 reduce-scatter.20
  1710.7 138.3 reduce-scatter.18
  1851.2 138.2 reduce-scatter.24
  1991.8 138.2 reduce-scatter.22
  2132.3 138.3 reduce-scatter.28
  2272.8 138.3 reduce-scatter.26
  2413.5 156.1 reduce-scatter.38
  2571.9 45.6 all-gather.40
  2619.7 45.5 all-gather.38
  2667.5 43.3 all-gather.44
  2713.0 41.1 all-gather.42
  2756.3 41.3 all-gather.48
  2800.4 41.3 all-gather.46
where the time goes:
time: 2860 us; the launch traced here: 2850 us
  waiting for transfers between devices  2190 us (77%)
  blocking collectives  337 us (12%)
  matrix products  140 us (5%)
  local copies, waits for them, and re-layouts  118 us (4%)
  other arithmetic  47.5 us (2%)
    reduce_scatter x2, waiting for transfers between devices, reduce_grads(): lax.psum_scatter(ordered[7], ('wide', 'narrow'), scatter_dimension=0, til...  310 us
    reduce_scatter x2, waiting for transfers between devices, reduce_grads(): lax.psum_scatter(ordered[2], ('wide', 'narrow'), scatter_dimension=0, til...  280 us
    reduce_scatter x2, waiting for transfers between devices, reduce_grads(): lax.psum_scatter(ordered[4], ('wide', 'narrow'), scatter_dimension=0, til...  279 us
    reduce_scatter x2, waiting for transfers between devices, reduce_grads(): lax.psum_scatter(ordered[3], ('wide', 'narrow'), scatter_dimension=0, til...  279 us
    reduce_scatter x2, waiting for transfers between devices, reduce_grads(): lax.psum_scatter(ordered[1], ('wide', 'narrow'), scatter_dimension=0, til...  216 us
    reduce_scatter x2, waiting for transfers between devices, reduce_grads(): lax.psum_scatter(ordered[8], ('wide', 'narrow'), scatter_dimension=0, til...  186 us
    reduce_scatter x2, waiting for transfers between devices, reduce_grads(): lax.psum_scatter(ordered[6], ('wide', 'narrow'), scatter_dimension=0, til...  137 us
    all_gather x2, waiting for transfers between devices, fetch_layer(): lax.all_gather(params[7][layer_index], 'narrow', axis=0, tiled=True)  83.1 us
  transfers between devices with their start and end apart: 34, of which 29 were waited for; matrix products, arithmetic and copies ran while one was open for 9% of the time, Pallas kernels for 0%

commit v1 on v0

--- a/solution.py
+++ b/solution.py
@@ -193,12 +193,9 @@
 
 
 def layer_backward(
-    stream, weights, first_values, values_extra, length, cos_table, sin_table, grad_result
+    stream, weights, first_values, values_extra, length, cos_table, sin_table, grad_result, saved
 ):
     gain_attn, w_query, w_key, w_value, w_out, gain_mlp, w_gate, w_up, w_down = weights
-    result, value_rows, saved = layer_forward(
-        stream, weights, first_values, length, cos_table, sin_table
-    )
     (
         inverse_attn,
         normed,
@@ -218,22 +215,18 @@
     width = HEADS * HEAD_DIM
     head_shape = (seq_len, HEADS, HEAD_DIM)
     grad_result_low = grad_result.astype(jnp.bfloat16)
-    grad_w_down = contract_rows(hidden, grad_result_low)
     grad_hidden = times_flip(grad_result_low, w_down)
     sigmoid_gate = jax.nn.sigmoid(gate_proj)
     grad_gate = (
         grad_hidden * up_proj * sigmoid_gate * (1.0 + gate_proj * (1.0 - sigmoid_gate))
     ).astype(jnp.bfloat16)
     grad_up = (grad_hidden * gate_proj * sigmoid_gate).astype(jnp.bfloat16)
-    grad_w_gate = contract_rows(normed_mid, grad_gate)
-    grad_w_up = contract_rows(normed_mid, grad_up)
     grad_normed_mid = times_flip(grad_gate, w_gate) + times_flip(grad_up, w_up)
     grad_middle, grad_gain_mlp = rms_back(
         middle, inverse_mlp, gain_mlp.astype(jnp.float32), grad_normed_mid
     )
     grad_middle = grad_middle + grad_result
     grad_middle_low = grad_middle.astype(jnp.bfloat16)
-    grad_w_out = contract_rows(attended_low, grad_middle_low)
     grad_attended = times_flip(grad_middle_low, w_out).astype(jnp.bfloat16).reshape(head_shape)
     grad_query_rot, grad_key_rot, grad_mixed = attention_backward(
         query_rows, key_rows, mixed_low, log_totals, grad_attended, length
@@ -253,9 +246,6 @@
     else:
         grad_value = (0.5 * grad_mixed).astype(jnp.bfloat16)
         extra_out = 0.5 * grad_mixed
-    grad_w_query = contract_rows(normed, grad_query)
-    grad_w_key = contract_rows(normed, grad_key)
-    grad_w_value = contract_rows(normed, grad_value)
     grad_normed = (
         times_flip(grad_query, w_query)
         + times_flip(grad_key, w_key)
@@ -265,86 +255,67 @@
         stream, inverse_attn, gain_attn.astype(jnp.float32), grad_normed
     )
     grad_stream = grad_stream + grad_middle
-    grads = (
-        grad_gain_attn,
-        grad_w_query,
-        grad_w_key,
-        grad_w_value,
-        grad_w_out,
-        grad_gain_mlp,
-        grad_w_gate,
-        grad_w_up,
-        grad_w_down,
-    )
-    return (grad_stream, grads, extra_out)
+    factors = (
+        normed,
+        attended_low,
+        normed_mid,
+        hidden,
+        grad_query,
+        grad_key,
+        grad_value,
+        grad_middle_low,
+        grad_gate,
+        grad_up,
+        grad_result_low,
+    )
+    return (grad_stream, factors, (grad_gain_attn, grad_gain_mlp), extra_out)
 
 
 def fetch_layer(params, layer_index):
-    return (
-        lax.all_gather(params[0][layer_index], "narrow", axis=0, tiled=True),
-        lax.all_gather(params[1][layer_index], "narrow", axis=0, tiled=True),
-        lax.all_gather(params[2][layer_index], "narrow", axis=0, tiled=True),
-        lax.all_gather(params[3][layer_index], "narrow", axis=0, tiled=True),
-        lax.all_gather(params[4][layer_index], "narrow", axis=0, tiled=True),
-        lax.all_gather(params[5][layer_index], "narrow", axis=0, tiled=True),
-        lax.all_gather(params[6][layer_index], "narrow", axis=0, tiled=True),
-        lax.all_gather(params[7][layer_index], "narrow", axis=0, tiled=True),
-        lax.all_gather(params[8][layer_index], "narrow", axis=0, tiled=True),
-    )
-
-
-def arrange_rows(grad_full, narrow_size, wide_size):
-    row_count = grad_full.shape[0]
-    parts = grad_full.reshape(
-        (narrow_size, wide_size, row_count // (narrow_size * wide_size)) + grad_full.shape[1:]
-    )
-    return jnp.swapaxes(parts, 0, 1).reshape(grad_full.shape)
-
-
-def reduce_grads(grads):
-    narrow_size = lax.axis_size("narrow")
-    wide_size = lax.axis_size("wide")
-    ordered = [arrange_rows(grad_full, narrow_size, wide_size) for grad_full in grads]
-    pieces = (
-        lax.psum_scatter(ordered[0], ("wide", "narrow"), scatter_dimension=0, tiled=True),
-        lax.psum_scatter(ordered[1], ("wide", "narrow"), scatter_dimension=0, tiled=True),
-        lax.psum_scatter(ordered[2], ("wide", "narrow"), scatter_dimension=0, tiled=True),
-        lax.psum_scatter(ordered[3], ("wide", "narrow"), scatter_dimension=0, tiled=True),
-        lax.psum_scatter(ordered[4], ("wide", "narrow"), scatter_dimension=0, tiled=True),
-        lax.psum_scatter(ordered[5], ("wide", "narrow"), scatter_dimension=0, tiled=True),
-        lax.psum_scatter(ordered[6], ("wide", "narrow"), scatter_dimension=0, tiled=True),
-        lax.psum_scatter(ordered[7], ("wide", "narrow"), scatter_dimension=0, tiled=True),
-        lax.psum_scatter(ordered[8], ("wide", "narrow"), scatter_dimension=0, tiled=True),
-    )
-    return (
-        lax.all_gather(pieces[0].astype(jnp.bfloat16), "wide", axis=0, tiled=True).astype(
-            jnp.float32
-        ),
-        lax.all_gather(pieces[1].astype(jnp.bfloat16), "wide", axis=0, tiled=True).astype(
-            jnp.float32
-        ),
-        lax.all_gather(pieces[2].astype(jnp.bfloat16), "wide", axis=0, tiled=True).astype(
-            jnp.float32
-        ),
-        lax.all_gather(pieces[3].astype(jnp.bfloat16), "wide", axis=0, tiled=True).astype(
-            jnp.float32
-        ),
-        lax.all_gather(pieces[4].astype(jnp.bfloat16), "wide", axis=0, tiled=True).astype(
-            jnp.float32
-        ),
-        lax.all_gather(pieces[5].astype(jnp.bfloat16), "wide", axis=0, tiled=True).astype(
-            jnp.float32
-        ),
-        lax.all_gather(pieces[6].astype(jnp.bfloat16), "wide", axis=0, tiled=True).astype(
-            jnp.float32
-        ),
-        lax.all_gather(pieces[7].astype(jnp.bfloat16), "wide", axis=0, tiled=True).astype(
-            jnp.float32
-        ),
-        lax.all_gather(pieces[8].astype(jnp.bfloat16), "wide", axis=0, tiled=True).astype(
-            jnp.float32
-        ),
-    )
+    return tuple(
+        lax.all_gather(param[layer_index], "narrow", axis=0, tiled=True) for param in params
+    )
+
+
+def share_columns(rows):
+    return lax.all_to_all(rows, "narrow", split_axis=1, concat_axis=0, tiled=True)
+
+
+def shard_grads(factors):
+    normed, attended, normed_mid, hidden = (share_columns(rows) for rows in factors[:4])
+    full = lax.all_gather(jnp.concatenate(factors[4:], axis=1), "narrow", axis=0, tiled=True)
+    width = HEADS * HEAD_DIM
+    inner = factors[8].shape[1]
+    cuts = [0]
+    for size in (3 * width, width, 2 * inner, width):
+        cuts.append(cuts[-1] + size)
+    parts = [full[:, a:b] for a, b in zip(cuts[:-1], cuts[1:])]
+    upper = jnp.concatenate(
+        [
+            contract_rows(normed, parts[0]).astype(jnp.bfloat16),
+            contract_rows(attended, parts[1]).astype(jnp.bfloat16),
+            contract_rows(normed_mid, parts[2]).astype(jnp.bfloat16),
+        ],
+        axis=1,
+    )
+    lower = contract_rows(hidden, parts[3]).astype(jnp.bfloat16)
+    return (upper, lower)
+
+
+def spread_grads(upper, lower, gain_grads, inner):
+    width = HEADS * HEAD_DIM
+    upper, lower = lax.psum((upper, lower), "wide")
+    gains = lax.psum_scatter(
+        jnp.stack(gain_grads), "narrow", scatter_dimension=1, tiled=True
+    )
+    gains = lax.psum(gains, "wide")
+    cuts = [0]
+    for size in (width, width, width, width, inner, inner):
+        cuts.append(cuts[-1] + size)
+    query, key, value, out, gate, up = (
+        upper[:, a:b].astype(jnp.float32) for a, b in zip(cuts[:-1], cuts[1:])
+    )
+    return (gains[0], query, key, value, out, gains[1], gate, up, lower.astype(jnp.float32))
 
 
 def shards(
@@ -364,44 +335,47 @@
     params = (gain_attn, w_query, w_key, w_value, w_out, gain_mlp, w_gate, w_up, w_down)
     seq_len = tokens.shape[0]
     length = lengths[0]
+    inner = w_gate.shape[2]
     cos_table, sin_table = rotary_tables(seq_len)
     start_stream = tokens.astype(jnp.float32)
     first_weights = fetch_layer(params, 0)
-    mid_stream, first_values, unused_saved = layer_forward(
+    mid_stream, first_values, first_saved = layer_forward(
         start_stream, first_weights, None, length, cos_table, sin_table
     )
     second_weights = fetch_layer(params, 1)
-    final_stream, unused_values, unused_later = layer_forward(
+    final_stream, unused_values, second_saved = layer_forward(
         mid_stream, second_weights, first_values, length, cos_table, sin_table
     )
     valid_rows = (jnp.arange(seq_len) < length).astype(jnp.float32)[:, None]
     grad_final = cotangent.astype(jnp.float32) * valid_rows
-    second_back = fetch_layer(params, 1)
-    grad_mid, grads_two, values_extra = layer_backward(
-        mid_stream, second_back, first_values, None, length, cos_table, sin_table, grad_final
-    )
-    reduced_two = reduce_grads(grads_two)
-    first_back = fetch_layer(params, 0)
-    grad_start, grads_one, unused_extra = layer_backward(
-        start_stream, first_back, None, values_extra, length, cos_table, sin_table, grad_mid
-    )
-    reduced_one = reduce_grads(grads_one)
+    grad_mid, factors_two, gains_two, values_extra = layer_backward(
+        mid_stream,
+        second_weights,
+        first_values,
+        None,
+        length,
+        cos_table,
+        sin_table,
+        grad_final,
+        second_saved,
+    )
+    reduced_two = spread_grads(*shard_grads(factors_two), gains_two, inner)
+    grad_start, factors_one, gains_one, unused_extra = layer_backward(
+        start_stream,
+        first_weights,
+        None,
+        values_extra,
+        length,
+        cos_table,
+        sin_table,
+        grad_mid,
+        first_saved,
+    )
+    reduced_one = spread_grads(*shard_grads(factors_one), gains_one, inner)
     stacked = [
         jnp.stack([one_part, two_part]) for one_part, two_part in zip(reduced_one, reduced_two)
     ]
-    return (
-        final_stream.astype(jnp.bfloat16),
-        grad_start,
-        stacked[0],
-        stacked[1],
-        stacked[2],
-        stacked[3],
-        stacked[4],
-        stacked[5],
-        stacked[6],
-        stacked[7],
-        stacked[8],
-    )
+    return (final_stream.astype(jnp.bfloat16), grad_start, *stacked)
 
 
 def solution(mesh):

time: 2860 us -> 1190 us (0.42)
  waiting for transfers between devices: 2190 us -> 867 us
  blocking collectives: 337 us -> 44 us
  local copies, waits for them, and re-layouts: 118 us -> 65.6 us
  starting transfers between devices: 2.03 us -> 32.9 us
    reduce_scatter x14 -> x0, waiting for transfers between devices: 1690 us -> none  [the longest x2 310 us: reduce_grads(): lax.psum_scatter(ordered[7], ('wide', 'narrow'), scatter_dimension=0, til...]
    psum x0 -> x1, waiting for transfers between devices: none -> 384 us  [spread_grads(): upper, lower = lax.psum((upper, lower), 'wide')]
    all_gather x12 -> x4, blocking collectives: 279 us -> 21.9 us  [fetch_layer(): lax.all_gather(param[layer_index], 'narrow', axis=0, tiled=True)]
    transpose x18 -> x0, local copies, waits for them, and re-layouts: 80.3 us -> none  [arrange_rows(): return jnp.swapaxes(parts, 0, 1).reshape(grad_full.shape)]
    unnamed x2 -> x0, blocking collectives: 58.7 us -> none
    all_gather x20 -> x16, waiting for transfers between devices: 499 us -> 455 us  [the longest x14 373 us: fetch_layer(): lax.all_gather(param[layer_index], 'narrow', axis=0, tiled=True)]
    all_to_all x0 -> x8, starting transfers between devices: none -> 32.2 us  [share_columns(): lax.all_to_all(rows, 'narrow', split_axis=1, concat_axis=0, tiled=True)]
  transfers between devices with their start and end apart: 34 -> 27, of which waited for: 29 -> 22; matrix products, arithmetic and copies ran while one was open for 9% -> 12% of each run, Pallas kernels for 0% -> 0%
where the time goes in v1:
time: 1190 us
  waiting for transfers between devices  867 us (73%)
  matrix products  123 us (10%)
  local copies, waits for them, and re-layouts  65.6 us (6%)
  blocking collectives  44 us (4%)
  other arithmetic  36.9 us (3%)
  starting transfers between devices  32.9 us (3%)
  between operations  16.2 us (1%)
    psum x1, waiting for transfers between devices, spread_grads(): upper, lower = lax.psum((upper, lower), 'wide')  384 us
    all_gather x14, waiting for transfers between devices, fetch_layer(): lax.all_gather(param[layer_index], 'narrow', axis=0, tiled=True)  373 us
    all_gather x2, waiting for transfers between devices, shard_grads(): lax.all_gather(jnp.concatenate(factors[4:], axis=1), 'narrow', axis=0, ti...  82.7 us
    dot_general x14, matrix products, matmul(): return jnp.dot(left, right, preferred_element_type=jnp.float32)  48 us
    dot_general x14, matrix products, times_flip(): lax.dot_general(left, right, (((1,), (1,)), ((), ())), preferred_element_...  35 us
    all_to_all x8, starting transfers between devices, share_columns(): lax.all_to_all(rows, 'narrow', split_axis=1, concat_axis=0, tiled=True)  32.2 us
    dot_general x8, matrix products, contract_rows(): lax.dot_general(left, right, (((0,), (0,)), ((), ())), preferred_element_...  29.8 us
    unnamed x200, local copies, waits for them, and re-layouts  27 us
  transfers between devices with their start and end apart: 27, of which 22 were waited for; matrix products, arithmetic and copies ran while one was open for 12% of the time, Pallas kernels for 0%

profile of v1, /device:TPU:0, one launch (start us, length us, event | category | flops | bytes accessed | tf_op | source)
XLA Modules:
  0.0 1185.2 jit_solution(16271846608518240800)
XLA Ops:
  17.4 3.9 fusion.164
  28.1 6.1 all-gather
  35.3 5.3 all-gather.5
  41.3 5.1 all-gather.9
  46.9 5.4 all-gather.14
  56.1 3.7 all-gather.39.cloned.1.call-done
  62.8 21.1 %all-gather.41.cloned.1.call-done = bf16[1,1024,1024]{2,1,0:T(8,128)(2,1)} async-done(((bf16[1,256,1024]{2,1,0:T(8,128)(2,1)}), bf16[1,1024,1024]{2,1,0:T(8,128)(2,1)}) %all-gather.41.cloned.1.call-update) | async-done | bytes 2097168 | tf_op jit(solution)/shard_map/all_gather | solution.py:276
  87.6 20.3 %all-gather.45.cloned.1.call-done = bf16[1,1024,1024]{2,1,0:T(8,128)(2,1)} async-done(((bf16[1,256,1024]{2,1,0:T(8,128)(2,1)}), bf16[1,1024,1024]{2,1,0:T(8,128)(2,1)}) %all-gather.45.cloned.1.call-update) | async-done | bytes 2097168 | tf_op jit(solution)/shard_map/all_gather | solution.py:276
  110.8 42.5 %all-gather.47.cloned.1.call-done = bf16[1,1024,2816]{2,1,0:T(8,128)(2,1)} async-done(((bf16[1,256,2816]{2,1,0:T(8,128)(2,1)}), bf16[1,1024,2816]{2,1,0:T(8,128)(2,1)}) %all-gather.47.cloned.1.call-update) | async-done | bytes 5767184 | tf_op jit(solution)/shard_map/all_gather | solution.py:276
  153.4 4.7 fusion.24
  158.0 40.7 %all-gather.49.cloned.1.call-done = bf16[1,1024,2816]{2,1,0:T(8,128)(2,1)} async-done(((bf16[1,256,2816]{2,1,0:T(8,128)(2,1)}), bf16[1,1024,2816]{2,1,0:T(8,128)(2,1)}) %all-gather.49.cloned.1.call-update) | async-done | bytes 5767184 | tf_op jit(solution)/shard_map/all_gather | solution.py:276
  198.8 5.3 multiply_convert_fusion.5
  204.1 40.2 %all-gather.51.cloned.1.call-done = bf16[1,2816,1024]{2,1,0:T(8,128)(2,1)} async-done(((bf16[1,704,1024]{2,1,0:T(8,128)(2,1)}), bf16[1,2816,1024]{2,1,0:T(8,128)(2,1)}) %all-gather.51.cloned.1.call-update) | async-done | bytes 5767184 | tf_op jit(solution)/shard_map/all_gather | solution.py:276
  244.3 3.6 multiply_reduce_fusion.9
  248.9 20.1 %all-gather.53.cloned.1.call-done = bf16[1,1024,1024]{2,1,0:T(8,128)(2,1)} async-done(((bf16[1,256,1024]{2,1,0:T(8,128)(2,1)}), bf16[1,1024,1024]{2,1,0:T(8,128)(2,1)}) %all-gather.53.cloned.1.call-update) | async-done | bytes 2097168 | tf_op jit(solution)/shard_map/all_gather | solution.py:276
  271.4 21.8 %all-gather.55.cloned.1.call-done = bf16[1,1024,1024]{2,1,0:T(8,128)(2,1)} async-done(((bf16[1,256,1024]{2,1,0:T(8,128)(2,1)}), bf16[1,1024,1024]{2,1,0:T(8,128)(2,1)}) %all-gather.55.cloned.1.call-update) | async-done | bytes 2097168 | tf_op jit(solution)/shard_map/all_gather | solution.py:276
  296.6 20.6 %all-gather.57.cloned.1.call-done = bf16[1,1024,1024]{2,1,0:T(8,128)(2,1)} async-done(((bf16[1,256,1024]{2,1,0:T(8,128)(2,1)}), bf16[1,1024,1024]{2,1,0:T(8,128)(2,1)}) %all-gather.57.cloned.1.call-update) | async-done | bytes 2097168 | tf_op jit(solution)/shard_map/all_gather | solution.py:276
  322.4 19.0 %all-gather.59.cloned.1.call-done = bf16[1,1024,1024]{2,1,0:T(8,128)(2,1)} async-done(((bf16[1,256,1024]{2,1,0:T(8,128)(2,1)}), bf16[1,1024,1024]{2,1,0:T(8,128)(2,1)}) %all-gather.59.cloned.1.call-update) | async-done | bytes 2097168 | tf_op jit(solution)/shard_map/all_gather | solution.py:276
  344.5 42.2 %all-gather.63.cloned.1.call-done = bf16[1,1024,2816]{2,1,0:T(8,128)(2,1)} async-done(((bf16[1,256,2816]{2,1,0:T(8,128)(2,1)}), bf16[1,1024,2816]{2,1,0:T(8,128)(2,1)}) %all-gather.63.cloned.1.call-update) | async-done | bytes 5767184 | tf_op jit(solution)/shard_map/all_gather | solution.py:276
  386.8 4.8 fusion.8
  391.5 40.8 %all-gather.65.cloned.1.call-done = bf16[1,2816,1024]{2,1,0:T(8,128)(2,1)} async-done(((bf16[1,704,1024]{2,1,0:T(8,128)(2,1)}), bf16[1,2816,1024]{2,1,0:T(8,128)(2,1)}) %all-gather.65.cloned.1.call-update) | async-done | bytes 5767184 | tf_op jit(solution)/shard_map/all_gather | solution.py:276
  432.3 6.1 fusion.2
  438.4 39.3 %all-gather.61.cloned.1.call-done = bf16[1,1024,2816]{2,1,0:T(8,128)(2,1)} async-done(((bf16[1,256,2816]{2,1,0:T(8,128)(2,1)}), bf16[1,1024,2816]{2,1,0:T(8,128)(2,1)}) %all-gather.61.cloned.1.call-update) | async-done | bytes 5767184 | tf_op jit(solution)/shard_map/all_gather | solution.py:276
  477.7 5.8 multiply_convert_fusion.3
  483.5 5.1 fusion.6
  505.5 5.5 multiply_convert_fusion.1
  552.6 4.0 all-to-all-start.2
  569.8 4.1 all-to-all-start
  573.8 43.9 %all-gather.35.cloned.1.call-done = bf16[512,10752]{1,0:T(8,128)(2,1)} async-done(((bf16[128,10752]{1,0:T(8,128)(2,1)}), bf16[512,10752]{1,0:T(8,128)(2,1)}) %all-gather.35.cloned.1.call-update) | async-done | bytes 11010064 | tf_op jit(solution)/shard_map/all_gather | solution.py:286
  617.7 4.4 convolution_convert_fusion.1
  622.2 4.0 all-to-all-start.1
  626.2 4.7 convolution_convert_fusion.3
  632.5 4.0 all-to-all-start.3
  639.1 6.7 all-to-all-done.3
  645.8 4.0 all-to-all-start.4
  649.8 4.2 pad_maximum_fusion
  654.1 5.1 all-to-all-done.4
  659.1 3.6 all-to-all-start.5
  662.7 38.8 %all-gather.37.cloned.1.call-done = bf16[512,10752]{1,0:T(8,128)(2,1)} async-done(((bf16[128,10752]{1,0:T(8,128)(2,1)}), bf16[512,10752]{1,0:T(8,128)(2,1)}) %all-gather.37.cloned.1.call-update) | async-done | bytes 11010064 | tf_op jit(solution)/shard_map/all_gather | solution.py:286
  701.5 4.1 convolution_convert_fusion.2
  705.6 4.2 all-to-all-start.6
  712.5 4.4 convolution_convert_fusion
  716.9 3.9 all-to-all-done.6
  720.8 4.2 all-to-all-start.7
  725.0 4.2 pad_maximum_fusion.1
  741.7 4.4 fusion.100
  750.5 22.1 %all-reduce = (f32[2,256]{1,0:T(2,128)S(1)}, f32[2,256]{1,0:T(2,128)S(1)}) all-reduce(f32[2,256]{1,0:T(2,128)S(1)} %copy.136, f32[2,256]{1,0:T(2,128)S(1)} %copy.134), channel_id=1, replica_groups=mesh['wide'=8,'narrow'=4] {'wide'}, use_global_device_ids=true, to_apply=%region_21.22 | all-reduce | flops 1024 | bytes 8192 | tf_op jit(solution)/shard_map/psum | solution.py:311
  773.8 384.0 %all-reduce.4.cloned.1.call-done = (bf16[256,9728]{1,0:T(8,128)(2,1)}, bf16[256,9728]{1,0:T(8,128)(2,1)}, bf16[1,704,1024]{2,1,0:T(8,128)(2,1)}, bf16[1,704,1024]{2,1,0:T(8,128)(2,1)}) async-done(((bf16[256,9728]{1,0:T(8,128)(2,1)}, bf16[256,9728]{1,0:T(8,128)(2,1)}, bf16[1,704,1024]{2,1,0:T(8,128)(2,1)}, bf16[1,704,1024]{2,1,0:T(8,128)(2,1)}), (bf16[256,9728]{1,0:T(8,128)(2,1)}, ...) | async-done | bytes 12845072 | tf_op jit(solution)/shard_map/psum | solution.py:307
  (375 shorter events, 162.7 us)
Async XLA Ops:
  7.2 46.4 %all-gather.43.cloned.1.call-start = ((), (), s32[]{:S(2)}) async-start(), calls=%async_computation.14 | async-start | bytes 2621440 | tf_op jit(solution)/shard_map/all_gather | solution.py:276
  9.6 50.2 %all-gather.39.cloned.1.call-start = ((), (), s32[]{:S(2)}) async-start(), calls=%async_computation.12 | async-start | bytes 2621440 | tf_op jit(solution)/shard_map/all_gather | solution.py:276
  10.7 73.2 %all-gather.41.cloned.1.call-start = ((), (), s32[]{:S(2)}) async-start(), calls=%async_computation.13 | async-start | bytes 2621440 | tf_op jit(solution)/shard_map/all_gather | solution.py:276
  13.2 94.7 %all-gather.45.cloned.1.call-start = ((), (), s32[]{:S(2)}) async-start(), calls=%async_computation.15 | async-start | bytes 2621440 | tf_op jit(solution)/shard_map/all_gather | solution.py:276
  15.5 137.8 %all-gather.47.cloned.1.call-start = ((), (), s32[]{:S(2)}) async-start(), calls=%async_computation.16 | async-start | bytes 7208960 | tf_op jit(solution)/shard_map/all_gather | solution.py:276
  17.4 181.4 %all-gather.49.cloned.1.call-start = ((), (), s32[]{:S(2)}) async-start(), calls=%async_computation.17 | async-start | bytes 7208960 | tf_op jit(solution)/shard_map/all_gather | solution.py:276
  21.4 223.0 %all-gather.51.cloned.1.call-start = ((), (), s32[]{:S(2)}) async-start(), calls=%async_computation.18 | async-start | bytes 7208960 | tf_op jit(solution)/shard_map/all_gather | solution.py:276
  23.3 245.8 %all-gather.53.cloned.1.call-start = ((), (), s32[]{:S(2)}) async-start(), calls=%async_computation.19 | async-start | bytes 2621440 | tf_op jit(solution)/shard_map/all_gather | solution.py:276
  24.0 269.2 %all-gather.55.cloned.1.call-start = ((), (), s32[]{:S(2)}) async-start(), calls=%async_computation.20 | async-start | bytes 2621440 | tf_op jit(solution)/shard_map/all_gather | solution.py:276
  24.8 9.5 copy-start.13
  24.8 292.4 %all-gather.57.cloned.1.call-start = ((), (), s32[]{:S(2)}) async-start(), calls=%async_computation.21 | async-start | bytes 2621440 | tf_op jit(solution)/shard_map/all_gather | solution.py:276
  25.4 9.9 copy-start.87
  25.4 316.0 %all-gather.59.cloned.1.call-start = ((), (), s32[]{:S(2)}) async-start(), calls=%async_computation.22 | async-start | bytes 2621440 | tf_op jit(solution)/shard_map/all_gather | solution.py:276
  26.1 360.6 %all-gather.63.cloned.1.call-start = ((), (), s32[]{:S(2)}) async-start(), calls=%async_computation.24 | async-start | bytes 7208960 | tf_op jit(solution)/shard_map/all_gather | solution.py:276
  26.7 405.6 %all-gather.65.cloned.1.call-start = ((), (), s32[]{:S(2)}) async-start(), calls=%async_computation.25 | async-start | bytes 7208960 | tf_op jit(solution)/shard_map/all_gather | solution.py:276
  27.5 450.3 %all-gather.61.cloned.1.call-start = ((), (), s32[]{:S(2)}) async-start(), calls=%async_computation.23 | async-start | bytes 7208960 | tf_op jit(solution)/shard_map/all_gather | solution.py:276
  28.0 589.7 %all-gather.35.cloned.1.call-start = ((), (), s32[]{:S(2)}) async-start(), calls=%async_computation.10 | async-start | bytes 13762560 | tf_op jit(solution)/shard_map/all_gather | solution.py:286
  34.3 19.3 %copy-start.75 = (f32[1,1024]{1,0:T(1,128)}, f32[1,1024]{1,0:T(1,128)S(1)}, u32[]{:S(2)}) copy-start(f32[1,1024]{1,0:T(1,128)S(1)} %convert_element_type.316) | copy-start | bytes 12292
  34.4 19.1 %copy-start.79 = (f32[128]{0:T(128)}, f32[128]{0:T(128)S(1)}, u32[]{:S(2)}) copy-start(f32[128]{0:T(128)S(1)} %add_rsqrt_fusion.3) | copy-start | bytes 1540
  62.8 24.5 %copy-start.64 = (bf16[128,1024]{0,1:T(8,128)(2,1)}, bf16[128,1024]{0,1:T(8,128)(2,1)S(1)}, u32[]{:S(2)}) copy-start(bf16[128,1024]{0,1:T(8,128)(2,1)S(1)} %copy.89) | copy-start | bytes 786436
  87.3 23.4 %copy-start.72 = (f32[1,1024]{1,0:T(1,128)S(1)}, f32[1,1024]{1,0:T(1,128)}, u32[]{:S(2)}) copy-start(f32[1,1024]{1,0:T(1,128)} %convert_element_type.317) | copy-start | bytes 12292
  87.6 70.4 %copy-start.68 = (bf16[16,64,128]{2,1,0:T(8,128)(2,1)}, bf16[16,64,128]{2,1,0:T(8,128)(2,1)S(1)}, u32[]{:S(2)}) copy-start(bf16[16,64,128]{2,1,0:T(8,128)(2,1)S(1)} %convolution_convert_fusion.9) | copy-start | bytes 786436
  110.1 47.9 %copy-start.81 = (f32[128]{0:T(128)}, f32[128]{0:T(128)S(1)}, u32[]{:S(2)}) copy-start(f32[128]{0:T(128)S(1)} %add_rsqrt_fusion.2) | copy-start | bytes 1540
  110.8 87.9 %copy-start.22 = (bf16[128,1024]{1,0:T(8,128)(2,1)}, bf16[128,1024]{1,0:T(8,128)(2,1)S(1)}, u32[]{:S(2)}) copy-start(bf16[128,1024]{1,0:T(8,128)(2,1)S(1)} %multiply_convert_fusion.10) | copy-start | bytes 786436
  204.1 43.9 %copy-start.29 = (bf16[128,2816]{1,0:T(8,128)(2,1)}, bf16[128,2816]{1,0:T(8,128)(2,1)S(1)}, u32[]{:S(2)}) copy-start(bf16[128,2816]{1,0:T(8,128)(2,1)S(1)} %get-tuple-element.204) | copy-start | bytes 2162692
  248.0 21.1 %copy-start.83 = (f32[128]{0:T(128)}, f32[128]{0:T(128)S(1)}, u32[]{:S(2)}) copy-start(f32[128]{0:T(128)S(1)} %add_rsqrt_fusion.1) | copy-start | bytes 1540
  248.9 68.3 %copy-start.16 = (bf16[128,1024]{1,0:T(8,128)(2,1)}, bf16[128,1024]{1,0:T(8,128)(2,1)S(1)}, u32[]{:S(2)}) copy-start(bf16[128,1024]{1,0:T(8,128)(2,1)S(1)} %multiply_convert_fusion.9) | copy-start | bytes 786436
  271.3 50.0 %copy-start.66 = (bf16[128,1024]{0,1:T(8,128)(2,1)}, bf16[128,1024]{0,1:T(8,128)(2,1)S(1)}, u32[]{:S(2)}) copy-start(bf16[128,1024]{0,1:T(8,128)(2,1)S(1)} %copy.93) | copy-start | bytes 786436
  322.4 21.3 %copy-start.74 = (f32[1,1024]{1,0:T(1,128)S(1)}, f32[1,1024]{1,0:T(1,128)}, u32[]{:S(2)}) copy-start(f32[1,1024]{1,0:T(1,128)} %convert_element_type.319) | copy-start | bytes 12292
  344.5 87.8 %copy-start.85 = (f32[128]{0:T(128)S(1)}, f32[128]{0:T(128)}, u32[]{:S(2)}) copy-start(f32[128]{0:T(128)} %fusion.161) | copy-start | bytes 1540
  504.9 10.7 copy-start.20
  517.2 17.2 %copy-start.9 = (f32[128,1024]{1,0:T(8,128)}, f32[128,1024]{1,0:T(8,128)S(1)}, u32[]{:S(2)}) copy-start(f32[128,1024]{1,0:T(8,128)S(1)} %subtract_add_fusion) | copy-start | bytes 1572868
  522.6 12.5 %copy-start.53 = (bf16[128,16,64]{0,2,1:T(8,128)(2,1)}, bf16[128,16,64]{0,2,1:T(8,128)(2,1)S(1)}, u32[]{:S(2)}) copy-start(bf16[128,16,64]{0,2,1:T(8,128)(2,1)S(1)} %get-tuple-element.178) | copy-start | bytes 786436
  529.1 8.9 copy-start.21
  538.8 8.7 copy-start.32
  538.8 162.7 %all-gather.37.cloned.1.call-start = ((), (), s32[]{:S(2)}) async-start(), calls=%async_computation.11 | async-start | bytes 13762560 | tf_op jit(solution)/shard_map/all_gather | solution.py:286
  549.3 9.4 copy-start.54
  552.6 17.1 %all-to-all-start.2 = ((bf16[128,4,256]{2,0,1:T(8,128)(2,1)}), bf16[128,4,256]{2,0,1:T(8,128)(2,1)}, u32[]{:S(2)}, u32[]{:S(2)}) async-start(bf16[128,4,256]{2,0,1:T(8,128)(2,1)} %bitcast.301), calls=%async_computation.2 | async-start | bytes 524288 | tf_op jit(solution)/shard_map/all_to_all | solution.py:281
  556.7 189.4 %reduce-scatter.7.cloned.1.call-start = ((), (), s32[]{:S(2)}) async-start(), calls=%async_computation.26 | async-start | bytes 655360
  564.0 185.5 %reduce-scatter.9.cloned.1.call-start = ((), (), s32[]{:S(2)}) async-start(), calls=%async_computation.27 | async-start | bytes 655360
  569.8 52.4 %all-to-all-start = ((bf16[128,4,256]{2,0,1:T(8,128)(2,1)}), bf16[128,4,256]{2,0,1:T(8,128)(2,1)}, u32[]{:S(2)}, u32[]{:S(2)}) async-start(bf16[128,4,256]{2,0,1:T(8,128)(2,1)} %bitcast.302), calls=%async_computation | async-start | bytes 524288 | tf_op jit(solution)/shard_map/all_to_all | solution.py:281
  622.2 10.3 all-to-all-start.1
  632.5 13.3 %all-to-all-start.3 = ((bf16[128,4,256]{2,0,1:T(8,128)(2,1)}), bf16[128,4,256]{2,0,1:T(8,128)(2,1)}, u32[]{:S(2)}, u32[]{:S(2)}) async-start(bf16[128,4,256]{2,0,1:T(8,128)(2,1)} %bitcast.348), calls=%async_computation.3 | async-start | bytes 524288 | tf_op jit(solution)/shard_map/all_to_all | solution.py:281
  645.8 13.3 %all-to-all-start.4 = ((bf16[128,4,256]{2,0,1:T(8,128)(2,1)}), bf16[128,4,256]{2,0,1:T(8,128)(2,1)}, u32[]{:S(2)}, u32[]{:S(2)}) async-start(bf16[128,4,256]{2,0,1:T(8,128)(2,1)} %copy.115), calls=%async_computation.4 | async-start | bytes 524288 | tf_op jit(solution)/shard_map/all_to_all | solution.py:281
  659.1 46.5 %all-to-all-start.5 = ((bf16[128,4,256]{2,0,1:T(8,128)(2,1)}), bf16[128,4,256]{2,0,1:T(8,128)(2,1)S(1)}, u32[]{:S(2)}, u32[]{:S(2)}) async-start(bf16[128,4,256]{2,0,1:T(8,128)(2,1)} %bitcast.347), calls=%async_computation.5 | async-start | bytes 524288 | tf_op jit(solution)/shard_map/all_to_all | solution.py:281
  705.6 15.2 %all-to-all-start.6 = ((bf16[128,4,704]{0,2,1:T(8,128)(2,1)}), bf16[128,4,704]{0,2,1:T(8,128)(2,1)}, u32[]{:S(2)}, u32[]{:S(2)}) async-start(bf16[128,4,704]{0,2,1:T(8,128)(2,1)} %bitcast.75), calls=%async_computation.6 | async-start | bytes 1441792 | tf_op jit(solution)/shard_map/all_to_all | solution.py:281
  720.8 15.2 %all-to-all-start.7 = ((bf16[128,4,704]{0,2,1:T(8,128)(2,1)}), bf16[128,4,704]{0,2,1:T(8,128)(2,1)}, u32[]{:S(2)}, u32[]{:S(2)}) async-start(bf16[128,4,704]{0,2,1:T(8,128)(2,1)} %bitcast.321), calls=%async_computation.7 | async-start | bytes 1441792 | tf_op jit(solution)/shard_map/all_to_all | solution.py:281
  725.0 432.9 %all-reduce.4.cloned.1.call-start = ((), (), s32[]{:S(2)}) async-start(), calls=%async_computation.28 | async-start | bytes 25690112 | tf_op jit(solution)/shard_map/psum | solution.py:307
  (72 other events, 239.2 us)
Sparse Core Ops, SparseCore 0:
  9.7 25.2 all-gather.42
  37.2 22.5 all-gather.38
  61.3 22.5 all-gather.40
  85.4 22.5 all-gather.44
  109.9 43.3 all-gather.46
  155.3 43.3 all-gather.48
  200.9 43.3 all-gather.50
  246.4 22.5 all-gather.52
  270.6 22.5 all-gather.54
  294.6 22.5 all-gather.56
  318.8 22.5 all-gather.58
  343.4 43.3 all-gather.62
  388.9 43.3 all-gather.64
  434.3 43.3 all-gather.60
  538.9 78.7 all-gather.34
  619.7 81.7 all-gather.36
  703.8 21.6 reduce-scatter.6
  727.9 21.6 reduce-scatter.8
  755.5 402.2 all-reduce.3
